TPU v7x, 256 devices: a whole 4x4x8 slice. The times are simulated.
256 devices in a mesh: grp: 8 (over z_hi, y), row: 32 (over z_lo, x, core).
Axes of the slice: x: 4, y: 4, z: 8 (z_hi: 2, z_lo: 4; z = z_hi * 4 + z_lo), core: 2. Of those that a mesh axis runs over, the one named last changes fastest.
Arguments:
- points: bfloat16 [524288, 128], P(('grp', 'row')), as said below
- centers: bfloat16 [8192, 128], replicated, as said below
- inner_factor: bfloat16 [8192, 8192], P('row'), as said below
- outer_factor: bfloat16 [8192, 8192], P('row'), as said below
- iterate: float32 [64, 8192], P(None, 'row'), may hold values from -6 to 6
- residual: float32 [64, 8192], P(None, 'row'), as said below
- direction: float32 [64, 8192], P(None, 'row'), as said below
Outputs:
- next_iterate: float32 [64, 8192], P(None, 'row')
- next_residual: float32 [64, 8192], P(None, 'row')
- next_direction: float32 [64, 8192], P(None, 'row')
Inputs may be any that keep to these rules, and one draw needn't show every extreme that they name: `inner_factor`: upper triangular: zero below the diagonal, positive on it. `outer_factor`: upper triangular: zero below the diagonal, positive on it. `residual`: finite real values. `direction`: finite real values. `points`: finite real values. `centers`: finite real values.
All inputs are finite; a program needn't handle non-finite values.
Results may differ from a plain program's by a relative error of at most 0.0056.
Values may be sent and summed in bfloat16 or wider, within the bound.
No kernel may reach another device: no remote copies, remote signals or barrier semaphores. Data moves between devices by JAX's collectives and lax.ppermute only.
A program may use at most 64 MiB of HBM per device.

v0:
```python
import jax
import jax.numpy as jnp
from jax import lax
from jax.sharding import PartitionSpec as P

ridge_weight = 0.5


def kernel_rows(block_points, centers, center_norms):
    point_wide = block_points.astype(jnp.float32)
    point_norms = jnp.sum(point_wide * point_wide, axis=1)
    cross_term = lax.dot_general(
        block_points, centers, (((1,), (1,)), ((), ())), preferred_element_type=jnp.float32
    )
    distance = point_norms[:, None] + center_norms[None, :] - 2.0 * cross_term
    return jnp.exp(distance * (-4.0 / block_points.shape[1])).astype(jnp.bfloat16)


def local(points, centers, inner_factor, outer_factor, iterate, residual, direction):
    contract_last = (((1,), (1,)), ((), ()))
    own_rows = inner_factor.shape[0]
    targets = direction.shape[0]
    direction_half = direction.astype(jnp.bfloat16)
    columns = inner_factor
    inner_term = lax.dot_general(
        lax.all_gather(direction_half, "row", axis=1, tiled=True),
        columns,
        contract_last,
        preferred_element_type=jnp.float32,
    )
    inner_half = inner_term.astype(jnp.bfloat16)
    columns = outer_factor
    outer_rows = lax.dot_general(
        lax.all_gather(inner_half, "row", axis=1, tiled=True),
        columns,
        contract_last,
        preferred_element_type=jnp.float32,
    )
    outer_half = lax.all_gather(outer_rows.astype(jnp.bfloat16), "row", axis=1, tiled=True)
    center_wide = centers.astype(jnp.float32)
    center_norms = jnp.sum(center_wide * center_wide, axis=1)
    local_points = points.shape[0]
    block_rows = min(512, local_points)
    point_blocks = points.reshape(local_points // block_rows, block_rows, points.shape[1])

    def one_block(carried, block_points):
        kernel_block = kernel_rows(block_points, centers, center_norms)
        fitted = lax.dot_general(
            outer_half, kernel_block, contract_last, preferred_element_type=jnp.float32
        ).astype(jnp.bfloat16)
        return (carried + jnp.dot(fitted, kernel_block, preferred_element_type=jnp.float32), None)

    partial_sums, _ = lax.scan(
        one_block, jnp.zeros((targets, centers.shape[0]), jnp.float32), point_blocks
    )
    summed_all = lax.psum(partial_sums, ("grp", "row"))
    own_normal = lax.dynamic_slice_in_dim(summed_all, lax.axis_index("row") * own_rows, own_rows, 1)
    normal_half = own_normal.astype(jnp.bfloat16)
    point_count = local_points * lax.axis_size("grp") * lax.axis_size("row")
    outer_terms = jnp.dot(normal_half, outer_factor, preferred_element_type=jnp.float32)
    shaped = (
        lax.psum_scatter(outer_terms, "row", scatter_dimension=1, tiled=True) / point_count
        + ridge_weight * inner_term
    )
    shaped_half = shaped.astype(jnp.bfloat16)
    inner_terms = jnp.dot(shaped_half, inner_factor, preferred_element_type=jnp.float32)
    operator_image = lax.psum_scatter(inner_terms, "row", scatter_dimension=1, tiled=True)
    old_norm = lax.psum(jnp.sum(residual * residual, axis=1), "row")
    curvature = lax.psum(jnp.sum(direction * operator_image, axis=1), "row")
    step_size = old_norm / curvature
    next_residual = residual - step_size[:, None] * operator_image
    new_norm = lax.psum(jnp.sum(next_residual * next_residual, axis=1), "row")
    next_iterate = iterate + step_size[:, None] * direction
    next_direction = next_residual + (new_norm / old_norm)[:, None] * direction
    return (next_iterate, next_residual, next_direction)


def solution(mesh):
    placed = (
        P(("grp", "row"), None),
        P(),
        P("row", None),
        P("row", None),
        P(None, "row"),
        P(None, "row"),
        P(None, "row"),
    )
    return jax.shard_map(
        local,
        mesh=mesh,
        in_specs=placed,
        out_specs=(P(None, "row"), P(None, "row"), P(None, "row")),
        check_vma=False,
    )
```

profile of v0, /device:TPU:1, one launch (start us, length us, event | category | flops | bytes accessed | tf_op | source)
XLA Modules:
  0.0 819.4 jit_solution(775019206389307324)
XLA Ops:
  7.2 0.0 all-gather.4.cloned.1.call-start
  7.2 1.5 convert_element_type.29
  8.7 0.0 all-gather.4.cloned.1.call-update
  8.7 0.0 all-gather.6.cloned.1.call-start
  8.7 66.0 %all-gather.4.cloned.1.call-done = bf16[64,8192]{1,0:T(8,128)(2,1)} async-done(((bf16[64,256]{1,0:T(8,128)(2,1)}), bf16[64,8192]{1,0:T(8,128)(2,1)}) %all-gather.4.cloned.1.call-update) | async-done | bytes 1048592 | tf_op jit(solution)/shard_map/all_gather | solution.py:26
  74.8 4.5 fusion.10
  79.3 0.0 all-gather.6.cloned.1.call-update
  79.3 0.0 all-gather.8.cloned.1.call-start
  79.4 59.4 %all-gather.6.cloned.1.call-done = bf16[64,8192]{1,0:T(8,128)(2,1)} async-done(((bf16[64,256]{1,0:T(8,128)(2,1)}), bf16[64,8192]{1,0:T(8,128)(2,1)}) %all-gather.6.cloned.1.call-update) | async-done | bytes 1048592 | tf_op jit(solution)/shard_map/all_gather | solution.py:34
  138.7 4.5 convolution_convert_fusion.1
  143.2 0.0 all-gather.8.cloned.1.call-update
  143.3 0.2 reduce-scatter.3.cloned.1.call-start
  143.5 2.7 multiply_reduce_fusion.1
  146.3 56.4 %all-gather.8.cloned.1.call-done = bf16[64,8192]{1,0:T(8,128)(2,1)} async-done(((bf16[64,256]{1,0:T(8,128)(2,1)}), bf16[64,8192]{1,0:T(8,128)(2,1)}) %all-gather.8.cloned.1.call-update) | async-done | bytes 1048592 | tf_op jit(solution)/shard_map/all_gather | solution.py:39
  202.7 87.9 %while.11 = (s32[]{:T(128)}, f32[64,8192]{1,0:T(8,128)S(1)}, bf16[4,512,128]{2,1,0:T(8,128)(2,1)}, f32[8192]{0:T(1024)S(1)}, bf16[8192,128]{1,0:T(8,128)(2,1)}, ...) while((s32[]{:T(128)}, f32[64,8192]{1,0:T(8,128)S(1)}, bf16[4,512,128]{2,1,0:T(8,128)(2,1)}, ...), condition=%wide.region_5.6_spmd.clone, body=%wide.region_3.0_spmd.clone.sunk | while | flops 2169732608 | bytes 28610700 | solution.py:53
  202.7 1.0 multiply_reduce_fusion.6
  203.7 0.0 copy-start
  203.7 9.0 %exponential_convert_fusion.2 = bf16[512,8192]{1,0:T(8,128)(2,1)} fusion(bf16[8192,128]{1,0:T(8,128)(2,1)} %get-tuple-element.134, f32[8192]{0:T(1024)S(1)} %get-tuple-element.133, f32[512]{0:T(512)S(1)} %multiply_reduce_fusion.6, bf16[4,512,128]{2,1,0:T(8,128)(2,1)} %get-tuple-element.132, s32[]{:T(128)S(6)} %copy.12), kind=kOutput, calls=%fused_computation.clone.1 | convolution fusion | flops 1094713344 | bytes 10651652 | tf_op jit(solution)/shard_map/while/body/eval_jaxpr/dot_general | solution.py:12
  212.8 0.0 copy-done
  212.8 11.9 %convolution_add_fusion.2 = f32[64,8192]{1,0:T(8,128)S(1)} fusion(bf16[512,8192]{1,0:T(8,128)(2,1)} %exponential_convert_fusion.2, f32[64,8192]{1,0:T(8,128)S(1)} %get-tuple-element.123, pred[]{:T(512)S(6)} %compare.3, bf16[64,8192]{1,0:T(8,128)(2,1)S(1)} %copy-done), kind=kOutput, calls=%fused_computation.1.clone.1 | convolution fusion | flops 1074823168 | bytes 13631489 | tf_op jit(solution)/shard_map/while/body/eval_jaxpr/dot_general | solution.py:51
  224.7 1.1 multiply_reduce_fusion.6
  225.7 0.0 copy-start
  225.7 9.0 %exponential_convert_fusion.2 = bf16[512,8192]{1,0:T(8,128)(2,1)} fusion(bf16[8192,128]{1,0:T(8,128)(2,1)} %get-tuple-element.134, f32[8192]{0:T(1024)S(1)} %get-tuple-element.133, f32[512]{0:T(512)S(1)} %multiply_reduce_fusion.6, bf16[4,512,128]{2,1,0:T(8,128)(2,1)} %get-tuple-element.132, s32[]{:T(128)S(6)} %copy.12), kind=kOutput, calls=%fused_computation.clone.1 | convolution fusion | flops 1094713344 | bytes 10651652 | tf_op jit(solution)/shard_map/while/body/eval_jaxpr/dot_general | solution.py:12
  234.8 0.0 copy-done
  234.8 11.9 %convolution_add_fusion.2 = f32[64,8192]{1,0:T(8,128)S(1)} fusion(bf16[512,8192]{1,0:T(8,128)(2,1)} %exponential_convert_fusion.2, f32[64,8192]{1,0:T(8,128)S(1)} %get-tuple-element.123, pred[]{:T(512)S(6)} %compare.3, bf16[64,8192]{1,0:T(8,128)(2,1)S(1)} %copy-done), kind=kOutput, calls=%fused_computation.1.clone.1 | convolution fusion | flops 1074823168 | bytes 13631489 | tf_op jit(solution)/shard_map/while/body/eval_jaxpr/dot_general | solution.py:51
  246.6 1.1 multiply_reduce_fusion.6
  247.7 0.0 copy-start
  247.7 9.0 %exponential_convert_fusion.2 = bf16[512,8192]{1,0:T(8,128)(2,1)} fusion(bf16[8192,128]{1,0:T(8,128)(2,1)} %get-tuple-element.134, f32[8192]{0:T(1024)S(1)} %get-tuple-element.133, f32[512]{0:T(512)S(1)} %multiply_reduce_fusion.6, bf16[4,512,128]{2,1,0:T(8,128)(2,1)} %get-tuple-element.132, s32[]{:T(128)S(6)} %copy.12), kind=kOutput, calls=%fused_computation.clone.1 | convolution fusion | flops 1094713344 | bytes 10651652 | tf_op jit(solution)/shard_map/while/body/eval_jaxpr/dot_general | solution.py:12
  256.7 0.0 copy-done
  256.7 11.9 %convolution_add_fusion.2 = f32[64,8192]{1,0:T(8,128)S(1)} fusion(bf16[512,8192]{1,0:T(8,128)(2,1)} %exponential_convert_fusion.2, f32[64,8192]{1,0:T(8,128)S(1)} %get-tuple-element.123, pred[]{:T(512)S(6)} %compare.3, bf16[64,8192]{1,0:T(8,128)(2,1)S(1)} %copy-done), kind=kOutput, calls=%fused_computation.1.clone.1 | convolution fusion | flops 1074823168 | bytes 13631489 | tf_op jit(solution)/shard_map/while/body/eval_jaxpr/dot_general | solution.py:51
  268.6 1.1 multiply_reduce_fusion.6
  269.7 0.0 copy-start
  269.7 9.0 %exponential_convert_fusion.2 = bf16[512,8192]{1,0:T(8,128)(2,1)} fusion(bf16[8192,128]{1,0:T(8,128)(2,1)} %get-tuple-element.134, f32[8192]{0:T(1024)S(1)} %get-tuple-element.133, f32[512]{0:T(512)S(1)} %multiply_reduce_fusion.6, bf16[4,512,128]{2,1,0:T(8,128)(2,1)} %get-tuple-element.132, s32[]{:T(128)S(6)} %copy.12), kind=kOutput, calls=%fused_computation.clone.1 | convolution fusion | flops 1094713344 | bytes 10651652 | tf_op jit(solution)/shard_map/while/body/eval_jaxpr/dot_general | solution.py:12
  278.7 0.0 copy-done
  278.7 11.9 %convolution_add_fusion.2 = f32[64,8192]{1,0:T(8,128)S(1)} fusion(bf16[512,8192]{1,0:T(8,128)(2,1)} %exponential_convert_fusion.2, f32[64,8192]{1,0:T(8,128)S(1)} %get-tuple-element.123, pred[]{:T(512)S(6)} %compare.3, bf16[64,8192]{1,0:T(8,128)(2,1)S(1)} %copy-done), kind=kOutput, calls=%fused_computation.1.clone.1 | convolution fusion | flops 1074823168 | bytes 13631489 | tf_op jit(solution)/shard_map/while/body/eval_jaxpr/dot_general | solution.py:51
  290.6 85.9 %all-reduce.2 = bf16[64,8192]{1,0:T(8,128)(2,1)S(1)} all-reduce(f32[64,8192]{1,0:T(8,128)S(1)} %get-tuple-element.35), channel_id=1, replica_groups=mesh['grp'=8,'row'=32] {'grp','row'}, use_global_device_ids=true, to_apply=%region_6.7 | all-reduce | flops 524288 | bytes 3145728 | tf_op jit(solution)/shard_map/psum | solution.py:56
  376.5 4.4 fusion.3
  380.9 0.0 reduce-scatter.3.cloned.1.call-update
  380.9 0.0 reduce-scatter.5.cloned.1.call-start
  380.9 139.3 %reduce-scatter.3.cloned.1.call-done = f32[64,256]{1,0:T(8,128)} async-done(((f32[64,8192]{1,0:T(8,128)}), f32[64,256]{1,0:T(8,128)}) %reduce-scatter.3.cloned.1.call-update) | async-done | bytes 65552 | tf_op jit(solution)/shard_map/reduce_scatter | solution.py:62
  520.3 0.0 copy-start.3
  520.3 0.0 copy-start.1
  520.3 0.0 copy-start.4
  520.3 4.5 fusion.4
  524.8 0.0 reduce-scatter.5.cloned.1.call-update
  524.8 0.0 copy-done.3
  524.8 0.1 multiply_reduce_fusion.4
  524.9 144.8 %reduce-scatter.5.cloned.1.call-done = f32[64,256]{1,0:T(8,128)} async-done(((f32[64,8192]{1,0:T(8,128)}), f32[64,256]{1,0:T(8,128)}) %reduce-scatter.5.cloned.1.call-update) | async-done | bytes 65552 | tf_op jit(solution)/shard_map/reduce_scatter | solution.py:67
  669.7 0.0 copy-done.1
  669.7 0.9 multiply_reduce_fusion.3
  670.7 72.6 %all-reduce = (f32[64]{0:T(128)S(1)}, f32[64]{0:T(128)S(1)}) all-reduce(f32[64]{0:T(128)S(1)} %multiply_reduce_fusion.4, f32[64]{0:T(128)S(1)} %multiply_reduce_fusion.3), channel_id=1, replica_groups=mesh['grp'=8,'row'=32] {'row'}, use_global_device_ids=true, to_apply=%region_1.2 | all-reduce | flops 128 | bytes 1024 | tf_op jit(solution)/shard_map/psum | solution.py:68
  743.2 1.0 multiply_reduce_fusion.2
  744.3 0.0 copy-start.2
  744.3 67.9 %psum.31 = f32[64]{0:T(128)S(1)} all-reduce(f32[64]{0:T(128)S(1)} %get-tuple-element.71), channel_id=1, replica_groups=mesh['grp'=8,'row'=32] {'row'}, use_global_device_ids=true, to_apply=%region_12.13 | all-reduce | flops 64 | bytes 512 | tf_op jit(solution)/shard_map/psum | solution.py:72
  812.1 0.0 copy-done.4
  812.1 0.7 multiply_add_fusion
  812.9 0.0 copy-done.2
  (3 shorter events, 0.0 us)
Async XLA Ops:
  7.2 67.6 %all-gather.4.cloned.1.call-start = ((), (), s32[]{:S(2)}) async-start(), calls=%async_computation.2 | async-start | bytes 1081344 | tf_op jit(solution)/shard_map/all_gather | solution.py:26
  8.7 130.0 %all-gather.6.cloned.1.call-start = ((), (), s32[]{:S(2)}) async-start(), calls=%async_computation.3 | async-start | bytes 1081344 | tf_op jit(solution)/shard_map/all_gather | solution.py:34
  79.3 123.4 %all-gather.8.cloned.1.call-start = ((), (), s32[]{:S(2)}) async-start(), calls=%async_computation.4 | async-start | bytes 1081344 | tf_op jit(solution)/shard_map/all_gather | solution.py:39
  143.3 377.0 %reduce-scatter.3.cloned.1.call-start = ((), (), s32[]{:S(2)}) async-start(), calls=%async_computation.5 | async-start | bytes 2162688 | tf_op jit(solution)/shard_map/reduce_scatter | solution.py:62
  203.7 9.1 %copy-start = (bf16[64,8192]{1,0:T(8,128)(2,1)S(1)}, bf16[64,8192]{1,0:T(8,128)(2,1)}, u32[]{:S(2)}) copy-start(bf16[64,8192]{1,0:T(8,128)(2,1)} %get-tuple-element.135) | copy-start | bytes 3145732 | tf_op jit(solution)/shard_map/while
  225.7 9.1 %copy-start = (bf16[64,8192]{1,0:T(8,128)(2,1)S(1)}, bf16[64,8192]{1,0:T(8,128)(2,1)}, u32[]{:S(2)}) copy-start(bf16[64,8192]{1,0:T(8,128)(2,1)} %get-tuple-element.135) | copy-start | bytes 3145732 | tf_op jit(solution)/shard_map/while
  247.7 9.1 %copy-start = (bf16[64,8192]{1,0:T(8,128)(2,1)S(1)}, bf16[64,8192]{1,0:T(8,128)(2,1)}, u32[]{:S(2)}) copy-start(bf16[64,8192]{1,0:T(8,128)(2,1)} %get-tuple-element.135) | copy-start | bytes 3145732 | tf_op jit(solution)/shard_map/while
  269.7 9.1 %copy-start = (bf16[64,8192]{1,0:T(8,128)(2,1)S(1)}, bf16[64,8192]{1,0:T(8,128)(2,1)}, u32[]{:S(2)}) copy-start(bf16[64,8192]{1,0:T(8,128)(2,1)} %get-tuple-element.135) | copy-start | bytes 3145732 | tf_op jit(solution)/shard_map/while
  380.9 288.8 %reduce-scatter.5.cloned.1.call-start = ((), (), s32[]{:S(2)}) async-start(), calls=%async_computation.6 | async-start | bytes 2162688 | tf_op jit(solution)/shard_map/reduce_scatter | solution.py:67
  520.3 4.5 copy-start.3
  520.3 149.4 %copy-start.1 = (f32[64,256]{1,0:T(8,128)S(1)}, f32[64,256]{1,0:T(8,128)}, u32[]{:S(2)}) copy-start(f32[64,256]{1,0:T(8,128)} %param.15) | copy-start | bytes 196612
  520.3 291.8 %copy-start.4 = (f32[64,256]{1,0:T(8,128)S(1)}, f32[64,256]{1,0:T(8,128)}, u32[]{:S(2)}) copy-start(f32[64,256]{1,0:T(8,128)} %param.13) | copy-start | bytes 196612
  744.3 68.6 %copy-start.2 = (f32[64,256]{1,0:T(8,128)}, f32[64,256]{1,0:T(8,128)S(1)}, u32[]{:S(2)}) copy-start(f32[64,256]{1,0:T(8,128)S(1)} %get-tuple-element.72) | copy-start | bytes 196612
Sparse Core Ops, SparseCore 0:
  10.3 64.4 all-gather.3
  79.4 59.2 all-gather.5
  143.4 59.2 all-gather.7
  381.0 139.2 reduce-scatter.2
  524.9 144.7 reduce-scatter.4
where the time goes:
time: 820 us; the launch traced here: 819 us
  waiting for transfers between devices  466 us (57%)
  blocking collectives  226 us (28%)
  matrix products  101 us (12%)
  between operations  13.8 us (2%)
  other arithmetic  11.2 us (1%)
    reduce_scatter x1, waiting for transfers between devices, local(): lax.psum_scatter(inner_terms, 'row', scatter_dimension=1, tiled=True)  145 us
    reduce_scatter x1, waiting for transfers between devices, local(): lax.psum_scatter(outer_terms, 'row', scatter_dimension=1, tiled=True)  139 us
    psum x1, blocking collectives, local(): summed_all = lax.psum(partial_sums, ('grp', 'row'))  85.9 us
    psum x1, blocking collectives, local(): old_norm = lax.psum(jnp.sum(residual * residual, axis=1), 'row')  72.6 us
    psum x1, blocking collectives, local(): new_norm = lax.psum(jnp.sum(next_residual * next_residual, axis=1), 'row')  67.9 us
    all_gather x1, waiting for transfers between devices, local(): lax.all_gather(direction_half, 'row', axis=1, tiled=True)  66 us
    all_gather x1, waiting for transfers between devices, local(): lax.all_gather(inner_half, 'row', axis=1, tiled=True)  59.4 us
    all_gather x1, waiting for transfers between devices, local(): lax.all_gather(outer_rows.astype(jnp.bfloat16), 'row', axis=1, tiled=True)  56.4 us
  transfers between devices with their start and end apart: 5, of which 5 were waited for; matrix products, arithmetic and copies ran while one was open for 0% of the time, Pallas kernels for 0%

commit v1 on v0

--- a/solution.py
+++ b/solution.py
@@ -36,7 +36,12 @@
         contract_last,
         preferred_element_type=jnp.float32,
     )
-    outer_half = lax.all_gather(outer_rows.astype(jnp.bfloat16), "row", axis=1, tiled=True)
+    outer_half = jnp.concatenate(
+        lax.all_to_all(
+            jnp.stack([outer_rows.astype(jnp.bfloat16)] * lax.axis_size("row")), "row", 0, 0
+        ),
+        axis=1,
+    )
     center_wide = centers.astype(jnp.float32)
     center_norms = jnp.sum(center_wide * center_wide, axis=1)
     local_points = points.shape[0]

time: 820 us -> 789 us (0.962)
  waiting for transfers between devices: 466 us -> 434 us
    all_gather x1 -> x0, waiting for transfers between devices: 56.4 us -> none  [local(): lax.all_gather(outer_rows.astype(jnp.bfloat16), 'row', axis=1, tiled=True)]
    all_to_all x0 -> x1, waiting for transfers between devices: none -> 23.8 us  [local(): lax.all_to_all(jnp.stack([outer_rows.astype(jnp.bfloat16)] * lax.axis_siz...]
where the time goes in v1:
time: 789 us; the launch traced here: 788 us
  waiting for transfers between devices  434 us (55%)
  blocking collectives  226 us (29%)
  matrix products  94.3 us (12%)
  between operations  13.8 us (2%)
  other arithmetic  11.2 us (1%)
    reduce_scatter x1, waiting for transfers between devices, local(): lax.psum_scatter(inner_terms, 'row', scatter_dimension=1, tiled=True)  145 us
    reduce_scatter x1, waiting for transfers between devices, local(): lax.psum_scatter(outer_terms, 'row', scatter_dimension=1, tiled=True)  140 us
    psum x1, blocking collectives, local(): summed_all = lax.psum(partial_sums, ('grp', 'row'))  85.5 us
    psum x1, blocking collectives, local(): old_norm = lax.psum(jnp.sum(residual * residual, axis=1), 'row')  72.6 us
    psum x1, blocking collectives, local(): new_norm = lax.psum(jnp.sum(next_residual * next_residual, axis=1), 'row')  67.8 us
    all_gather x1, waiting for transfers between devices, local(): lax.all_gather(direction_half, 'row', axis=1, tiled=True)  66 us
    all_gather x1, waiting for transfers between devices, local(): lax.all_gather(inner_half, 'row', axis=1, tiled=True)  59.4 us
    dot_general x4, matrix products, one_block(): jnp.dot(fitted, kernel_block, preferred_element_type=jnp.float32)  41.1 us
  transfers between devices with their start and end apart: 5, of which 5 were waited for; matrix products, arithmetic and copies ran while one was open for 0% of the time, Pallas kernels for 0%

profile of v1, /device:TPU:1, one launch (start us, length us, event | category | flops | bytes accessed | tf_op | source)
XLA Modules:
  0.0 788.3 jit_solution(9920850863537549509)
XLA Ops:
  7.2 0.0 all-gather.3.cloned.1.call-start
  7.2 1.5 convert_element_type.29
  8.7 0.0 all-gather.3.cloned.1.call-update
  8.7 0.0 all-gather.5.cloned.1.call-start
  8.7 66.0 %all-gather.3.cloned.1.call-done = bf16[64,8192]{1,0:T(8,128)(2,1)} async-done(((bf16[64,256]{1,0:T(8,128)(2,1)}), bf16[64,8192]{1,0:T(8,128)(2,1)}) %all-gather.3.cloned.1.call-update) | async-done | bytes 1048592 | tf_op jit(solution)/shard_map/all_gather | solution.py:26
  74.8 4.5 fusion.10
  79.3 0.0 all-gather.5.cloned.1.call-update
  79.3 59.4 %all-gather.5.cloned.1.call-done = bf16[64,8192]{1,0:T(8,128)(2,1)} async-done(((bf16[64,256]{1,0:T(8,128)(2,1)}), bf16[64,8192]{1,0:T(8,128)(2,1)}) %all-gather.5.cloned.1.call-update) | async-done | bytes 1048592 | tf_op jit(solution)/shard_map/all_gather | solution.py:34
  138.7 3.9 convolution_convert_fusion.1
  142.6 1.1 stack.2
  143.7 5.3 all-to-all-start
  149.0 0.0 reduce-scatter.3.cloned.1.call-start
  149.1 2.7 multiply_reduce_fusion.1
  151.8 23.8 %all-to-all-done = bf16[32,64,256]{2,1,0:T(8,128)(2,1)S(1)} async-done(((bf16[32,64,256]{2,1,0:T(8,128)(2,1)}), bf16[32,64,256]{2,1,0:T(8,128)(2,1)S(1)}, u32[]{:S(2)}, u32[]{:S(2)}) %all-to-all-start) | async-done | bytes 1048608 | tf_op jit(solution)/shard_map/all_to_all | solution.py:40
  175.7 0.0 copy-start
  175.7 1.0 copy-done
  176.7 1.3 copy.11
  178.0 81.3 %while.11 = (s32[]{:T(128)}, f32[64,8192]{1,0:T(8,128)S(1)}, bf16[4,512,128]{2,1,0:T(8,128)(2,1)}, f32[8192]{0:T(1024)S(1)}, bf16[8192,128]{1,0:T(8,128)(2,1)}, ...) while((s32[]{:T(128)}, f32[64,8192]{1,0:T(8,128)S(1)}, bf16[4,512,128]{2,1,0:T(8,128)(2,1)}, ...), condition=%wide.region_5.6_spmd.clone, body=%wide.region_3.0_spmd.clone.sunk | while | flops 2169732608 | bytes 24416368 | solution.py:58
  178.0 1.1 multiply_reduce_fusion.6
  179.0 9.0 %exponential_convert_fusion.2 = bf16[512,8192]{1,0:T(8,128)(2,1)} fusion(bf16[8192,128]{1,0:T(8,128)(2,1)} %get-tuple-element.134, f32[8192]{0:T(1024)S(1)} %get-tuple-element.133, f32[512]{0:T(512)S(1)} %multiply_reduce_fusion.6, bf16[4,512,128]{2,1,0:T(8,128)(2,1)} %get-tuple-element.132, s32[]{:T(128)S(6)} %copy.14), kind=kOutput, calls=%fused_computation.clone.1 | convolution fusion | flops 1094713344 | bytes 10651652 | tf_op jit(solution)/shard_map/while/body/eval_jaxpr/dot_general | solution.py:12
  188.0 10.3 %convolution_add_fusion.2 = f32[64,8192]{1,0:T(8,128)S(1)} fusion(bf16[512,8192]{1,0:T(8,128)(2,1)} %exponential_convert_fusion.2, f32[64,8192]{1,0:T(8,128)S(1)} %get-tuple-element.123, pred[]{:T(512)S(6)} %compare.3, bf16[64,8192]{1,0:T(8,128)(2,1)S(1)} %get-tuple-element.135), kind=kOutput, calls=%fused_computation.1.clone.1 | convolution fusion | flops 1074823168 | bytes 13631489 | tf_op jit(solution)/shard_map/while/body/eval_jaxpr/dot_general | solution.py:56
  198.3 1.1 multiply_reduce_fusion.6
  199.4 9.0 %exponential_convert_fusion.2 = bf16[512,8192]{1,0:T(8,128)(2,1)} fusion(bf16[8192,128]{1,0:T(8,128)(2,1)} %get-tuple-element.134, f32[8192]{0:T(1024)S(1)} %get-tuple-element.133, f32[512]{0:T(512)S(1)} %multiply_reduce_fusion.6, bf16[4,512,128]{2,1,0:T(8,128)(2,1)} %get-tuple-element.132, s32[]{:T(128)S(6)} %copy.14), kind=kOutput, calls=%fused_computation.clone.1 | convolution fusion | flops 1094713344 | bytes 10651652 | tf_op jit(solution)/shard_map/while/body/eval_jaxpr/dot_general | solution.py:12
  208.3 10.3 %convolution_add_fusion.2 = f32[64,8192]{1,0:T(8,128)S(1)} fusion(bf16[512,8192]{1,0:T(8,128)(2,1)} %exponential_convert_fusion.2, f32[64,8192]{1,0:T(8,128)S(1)} %get-tuple-element.123, pred[]{:T(512)S(6)} %compare.3, bf16[64,8192]{1,0:T(8,128)(2,1)S(1)} %get-tuple-element.135), kind=kOutput, calls=%fused_computation.1.clone.1 | convolution fusion | flops 1074823168 | bytes 13631489 | tf_op jit(solution)/shard_map/while/body/eval_jaxpr/dot_general | solution.py:56
  218.6 1.1 multiply_reduce_fusion.6
  219.7 9.0 %exponential_convert_fusion.2 = bf16[512,8192]{1,0:T(8,128)(2,1)} fusion(bf16[8192,128]{1,0:T(8,128)(2,1)} %get-tuple-element.134, f32[8192]{0:T(1024)S(1)} %get-tuple-element.133, f32[512]{0:T(512)S(1)} %multiply_reduce_fusion.6, bf16[4,512,128]{2,1,0:T(8,128)(2,1)} %get-tuple-element.132, s32[]{:T(128)S(6)} %copy.14), kind=kOutput, calls=%fused_computation.clone.1 | convolution fusion | flops 1094713344 | bytes 10651652 | tf_op jit(solution)/shard_map/while/body/eval_jaxpr/dot_general | solution.py:12
  228.7 10.3 %convolution_add_fusion.2 = f32[64,8192]{1,0:T(8,128)S(1)} fusion(bf16[512,8192]{1,0:T(8,128)(2,1)} %exponential_convert_fusion.2, f32[64,8192]{1,0:T(8,128)S(1)} %get-tuple-element.123, pred[]{:T(512)S(6)} %compare.3, bf16[64,8192]{1,0:T(8,128)(2,1)S(1)} %get-tuple-element.135), kind=kOutput, calls=%fused_computation.1.clone.1 | convolution fusion | flops 1074823168 | bytes 13631489 | tf_op jit(solution)/shard_map/while/body/eval_jaxpr/dot_general | solution.py:56
  239.0 1.1 multiply_reduce_fusion.6
  240.0 9.0 %exponential_convert_fusion.2 = bf16[512,8192]{1,0:T(8,128)(2,1)} fusion(bf16[8192,128]{1,0:T(8,128)(2,1)} %get-tuple-element.134, f32[8192]{0:T(1024)S(1)} %get-tuple-element.133, f32[512]{0:T(512)S(1)} %multiply_reduce_fusion.6, bf16[4,512,128]{2,1,0:T(8,128)(2,1)} %get-tuple-element.132, s32[]{:T(128)S(6)} %copy.14), kind=kOutput, calls=%fused_computation.clone.1 | convolution fusion | flops 1094713344 | bytes 10651652 | tf_op jit(solution)/shard_map/while/body/eval_jaxpr/dot_general | solution.py:12
  249.0 10.3 %convolution_add_fusion.2 = f32[64,8192]{1,0:T(8,128)S(1)} fusion(bf16[512,8192]{1,0:T(8,128)(2,1)} %exponential_convert_fusion.2, f32[64,8192]{1,0:T(8,128)S(1)} %get-tuple-element.123, pred[]{:T(512)S(6)} %compare.3, bf16[64,8192]{1,0:T(8,128)(2,1)S(1)} %get-tuple-element.135), kind=kOutput, calls=%fused_computation.1.clone.1 | convolution fusion | flops 1074823168 | bytes 13631489 | tf_op jit(solution)/shard_map/while/body/eval_jaxpr/dot_general | solution.py:56
  259.3 85.5 %all-reduce.2 = bf16[64,8192]{1,0:T(8,128)(2,1)S(1)} all-reduce(f32[64,8192]{1,0:T(8,128)S(1)} %get-tuple-element.35), channel_id=1, replica_groups=mesh['grp'=8,'row'=32] {'grp','row'}, use_global_device_ids=true, to_apply=%region_6.7 | all-reduce | flops 524288 | bytes 3145728 | tf_op jit(solution)/shard_map/psum | solution.py:61
  344.7 4.4 fusion.3
  349.1 0.0 reduce-scatter.3.cloned.1.call-update
  349.2 0.0 reduce-scatter.5.cloned.1.call-start
  349.2 140.0 %reduce-scatter.3.cloned.1.call-done = f32[64,256]{1,0:T(8,128)} async-done(((f32[64,8192]{1,0:T(8,128)}), f32[64,256]{1,0:T(8,128)}) %reduce-scatter.3.cloned.1.call-update) | async-done | bytes 65552 | tf_op jit(solution)/shard_map/reduce_scatter | solution.py:67
  489.2 0.0 copy-start.3
  489.2 0.0 copy-start.1
  489.3 0.0 copy-start.4
  489.3 4.5 fusion.4
  493.7 0.0 reduce-scatter.5.cloned.1.call-update
  493.7 0.0 copy-done.3
  493.7 0.1 multiply_reduce_fusion.4
  493.9 144.8 %reduce-scatter.5.cloned.1.call-done = f32[64,256]{1,0:T(8,128)} async-done(((f32[64,8192]{1,0:T(8,128)}), f32[64,256]{1,0:T(8,128)}) %reduce-scatter.5.cloned.1.call-update) | async-done | bytes 65552 | tf_op jit(solution)/shard_map/reduce_scatter | solution.py:72
  638.6 0.0 copy-done.1
  638.6 0.9 multiply_reduce_fusion.3
  639.6 72.6 %all-reduce = (f32[64]{0:T(128)S(1)}, f32[64]{0:T(128)S(1)}) all-reduce(f32[64]{0:T(128)S(1)} %multiply_reduce_fusion.4, f32[64]{0:T(128)S(1)} %multiply_reduce_fusion.3), channel_id=1, replica_groups=mesh['grp'=8,'row'=32] {'row'}, use_global_device_ids=true, to_apply=%region_1.2 | all-reduce | flops 128 | bytes 1024 | tf_op jit(solution)/shard_map/psum | solution.py:73
  712.2 1.0 multiply_reduce_fusion.2
  713.2 0.0 copy-start.2
  713.2 67.8 %psum.31 = f32[64]{0:T(128)S(1)} all-reduce(f32[64]{0:T(128)S(1)} %get-tuple-element.71), channel_id=1, replica_groups=mesh['grp'=8,'row'=32] {'row'}, use_global_device_ids=true, to_apply=%region_12.13 | all-reduce | flops 64 | bytes 512 | tf_op jit(solution)/shard_map/psum | solution.py:77
  781.1 0.0 copy-done.4
  781.1 0.7 multiply_add_fusion
  781.8 0.0 copy-done.2
  (3 shorter events, 0.0 us)
Async XLA Ops:
  7.2 67.6 %all-gather.3.cloned.1.call-start = ((), (), s32[]{:S(2)}) async-start(), calls=%async_computation.3 | async-start | bytes 1081344 | tf_op jit(solution)/shard_map/all_gather | solution.py:26
  8.7 130.0 %all-gather.5.cloned.1.call-start = ((), (), s32[]{:S(2)}) async-start(), calls=%async_computation.4 | async-start | bytes 1081344 | tf_op jit(solution)/shard_map/all_gather | solution.py:34
  143.7 31.9 %all-to-all-start = ((bf16[32,64,256]{2,1,0:T(8,128)(2,1)}), bf16[32,64,256]{2,1,0:T(8,128)(2,1)S(1)}, u32[]{:S(2)}, u32[]{:S(2)}) async-start(bf16[32,64,256]{2,1,0:T(8,128)(2,1)} %stack.2), calls=%async_computation | async-start | bytes 2097152 | tf_op jit(solution)/shard_map/all_to_all | solution.py:40
  149.0 340.2 %reduce-scatter.3.cloned.1.call-start = ((), (), s32[]{:S(2)}) async-start(), calls=%async_computation.5 | async-start | bytes 2162688 | tf_op jit(solution)/shard_map/reduce_scatter | solution.py:67
  175.7 1.0 copy-start
  349.2 289.5 %reduce-scatter.5.cloned.1.call-start = ((), (), s32[]{:S(2)}) async-start(), calls=%async_computation.6 | async-start | bytes 2162688 | tf_op jit(solution)/shard_map/reduce_scatter | solution.py:72
  489.2 4.5 copy-start.3
  489.2 149.4 %copy-start.1 = (f32[64,256]{1,0:T(8,128)S(1)}, f32[64,256]{1,0:T(8,128)}, u32[]{:S(2)}) copy-start(f32[64,256]{1,0:T(8,128)} %param.15) | copy-start | bytes 196612
  489.3 291.8 %copy-start.4 = (f32[64,256]{1,0:T(8,128)S(1)}, f32[64,256]{1,0:T(8,128)}, u32[]{:S(2)}) copy-start(f32[64,256]{1,0:T(8,128)} %param.13) | copy-start | bytes 196612
  713.2 68.6 %copy-start.2 = (f32[64,256]{1,0:T(8,128)}, f32[64,256]{1,0:T(8,128)S(1)}, u32[]{:S(2)}) copy-start(f32[64,256]{1,0:T(8,128)S(1)} %get-tuple-element.72) | copy-start | bytes 196612
Sparse Core Ops, SparseCore 0:
  10.3 64.4 all-gather.2
  79.4 59.2 all-gather.4
  349.3 139.9 reduce-scatter.2
  493.9 144.7 reduce-scatter.4
